TPU v7x, 256 devices: a whole 4x4x8 slice. The times are simulated.
256 devices in a mesh: src: 32 (over z, x), tgt: 8 (over y, core).
Axes of the slice: x: 4, y: 4, z: 8, core: 2. Of those that a mesh axis runs over, the one named last changes fastest.
Arguments:
- src_embed: float32 [65536, 256], P(('src', 'tgt')), may hold values from -7.5 to 7.5
- tgt_embed: float32 [32768, 256], P(('tgt', 'src')), may hold values from -7.5 to 7.5
- log_src: float32 [65536], P('src'), may hold values from -1.25 to 2.35
- log_tgt: float32 [32768], P('tgt'), may hold values from -1.25 to 2.35
- tgt_pot: float32 [32768], P('tgt'), may hold values from -1 to 6
Outputs:
- src_dual: float32 [65536], P('src')
- tgt_dual: float32 [32768], P('tgt')
All inputs are finite; a program needn't handle non-finite values.
Results may differ from a plain program's by a relative error of at most 0.0003.
Values sent between devices are 32-bit elements; how exact they have to be, the bound alone decides.
No kernel may reach another device: no remote copies, remote signals or barrier semaphores. Data moves between devices by JAX's collectives and lax.ppermute only.
A program may use at most 128 MiB of HBM per device.

v0:
```python
import functools
import math

import jax
import jax.numpy as jnp
from jax import lax
from jax.experimental import pallas as pl
from jax.experimental.pallas import tpu as pltpu
from jax.sharding import Mesh
from jax.sharding import PartitionSpec as P


EPSILON = 0.05
LOG2E = math.log2(math.e)
LN2 = math.log(2.0)
ZN, XN, YN, CN = 8, 4, 4, 2
ROW_TILE = 512
ROW_VMEM = 6 * 2**20
GROUP = 4
VMEM = pl.BlockSpec(memory_space=pltpu.VMEM)


def shift(value, axis, size, back):
    return lax.ppermute(value, axis, [(i, (i - back) % size) for i in range(size)])


def split(value):
    high = value.astype(jnp.bfloat16)
    return high, (value - high.astype(jnp.float32)).astype(jnp.bfloat16)


def nt_dot(left, right):
    return lax.dot_general(left, right, (((1,), (1,)), ((), ())), preferred_element_type=jnp.float32)


def to_column(row):
    return jnp.transpose(jnp.broadcast_to(row, (128, 128)))


def to_row(column):
    return jnp.transpose(jnp.broadcast_to(column, (128, 128)))[0:1, :]


def pack_source_kernel(width, own_ref, other_ref, s_ref, norm_ref):
    y, core = lax.axis_index("y"), lax.axis_index("c")
    scale = 2.0 * LOG2E / (width * EPSILON)
    for ref, side in ((own_ref, core), (other_ref, 1 - core)):
        for m in range(YN):
            rows = ref[m * 256:(m + 1) * 256, :]
            place = lax.rem(y + m, YN) * 2 + side
            high, low = split(rows * scale)
            where = pl.ds(pl.multiple_of(place * 256, 256), 256)
            s_ref[where, 0:256] = high
            s_ref[where, 256:512] = low
            norm = jnp.sum(rows * rows, axis=1, keepdims=True)
            for h in range(2):
                norm_ref[pl.ds(place * 2 + h, 1), :] = to_row(norm[h * 128:(h + 1) * 128, :])


def row_pass_kernel(width, offsets, first, group, *refs):
    count = len(offsets)
    s_ref, base_ref = refs[:2]
    refs = refs[2:]
    if not first:
        before_ref, refs = refs[0], refs[1:]
    *t_refs, u_out, tnorm_out, lse_out, t_scr, col_ref = refs
    z, x = lax.axis_index("z"), lax.axis_index("x")
    start = 0
    for ref in t_refs:
        for b in range(ref.shape[0] // 128):
            at = slice(start * 128, (start + 1) * 128)
            t = ref[b * 128:(b + 1) * 128, :]
            high, low = split(t)
            t_scr[at, 0:256] = high
            t_scr[at, 256:512] = low
            row = to_row(jnp.sum(t * t, axis=1, keepdims=True))
            tnorm_out[start:start + 1, :] = row
            k, m = offsets[start]
            place = lax.rem(z + k, ZN) * XN + lax.rem(x + m, XN)
            col_ref[at, :] = to_column((base_ref[pl.ds(place, 1), :] - row / (width * EPSILON)) * LOG2E)
            start += 1

    def tiles(g, carry):
        base = g * (group * ROW_TILE) if isinstance(g, int) else pl.multiple_of(g * (group * ROW_TILE), group * ROW_TILE)

        def product(i):
            at = pl.ds(base + i * ROW_TILE, ROW_TILE)
            high, low = s_ref[at, 0:256], s_ref[at, 256:512]
            t_high, t_low = t_scr[:, 0:256], t_scr[:, 256:512]
            u_out[:, at] = nt_dot(t_high, high) + nt_dot(t_high, low) + nt_dot(t_low, high)

        def totals(i):
            for h in range(ROW_TILE // 128):
                part = i * (ROW_TILE // 128) + h
                at = pl.ds(g * (group * ROW_TILE // 128) + part, 1)
                v = (u_out[:, pl.ds(base + part * 128, 128)] + col_ref[...]).reshape(count * 16, 8, 128)
                top = jnp.max(jnp.max(v, axis=0), axis=0, keepdims=True)
                total = jnp.sum(jnp.sum(jnp.exp2(v - top[None]), axis=0), axis=0, keepdims=True)
                if not first:
                    old = before_ref[at, :]
                    new_top = jnp.maximum(top, old)
                    total = total * jnp.exp2(top - new_top) + jnp.exp2(old - new_top)
                    top = new_top
                lse_out[at, :] = top + jnp.log2(total)

        product(0)
        for i in range(1, group):
            product(i)
            totals(i - 1)
        totals(group - 1)
        return carry

    groups = s_ref.shape[0] // (group * ROW_TILE)
    if groups == 1:
        tiles(0, 0)
    else:
        lax.fori_loop(0, groups, tiles, 0)


def column_pass_kernel(width, offsets, *refs):
    chunks = len(offsets)
    lse_refs, (log_ref, norm_ref) = refs[:YN], refs[YN:YN + 2]
    refs = refs[YN + 2:]
    tnorm_refs, u_refs = refs[:chunks], refs[chunks:2 * chunks]
    dual_out, col_out, d_ref, top_ref, total_ref = refs[2 * chunks:]
    z, x = lax.axis_index("z"), lax.axis_index("x")
    wide = u_refs[0].shape[1] // 128

    parts = jnp.stack([ref[...] for ref in lse_refs])
    lse = join(parts)
    dual_out[...] = norm_ref[...] / width - (EPSILON * LN2) * lse
    shifted = log_ref[...] * LOG2E - lse
    for r in range(wide):
        d_ref[:, r * 128:(r + 1) * 128] = jnp.broadcast_to(shifted[r:r + 1, :], (8, 128))

    def tree(op, values):
        while len(values) > 1:
            values = [op(values[k], values[k + 1]) for k in range(0, len(values), 2)]
        return values[0]

    for u_ref, tnorm_ref, places in zip(u_refs, tnorm_refs, offsets):
        def blocks(g, carry, u_ref=u_ref, tnorm_ref=tnorm_ref, places=places):
            def scan(b):
                for t in range(b * 16, (b + 1) * 16):
                    at = pl.ds(pl.multiple_of(g * GROUP * 128, 128) + t * 8, 8)
                    v = [u_ref[at, r * 128:(r + 1) * 128] + d_ref[:, r * 128:(r + 1) * 128] for r in range(wide)]
                    top = tree(jnp.maximum, v)
                    top_ref[t * 8:(t + 1) * 8, :] = top
                    total_ref[t * 8:(t + 1) * 8, :] = tree(jnp.add, [jnp.exp2(e - top) for e in v])

            def finish(b):
                tops = jnp.transpose(top_ref[b * 128:(b + 1) * 128, :])
                totals = jnp.transpose(total_ref[b * 128:(b + 1) * 128, :])
                top = jnp.max(tops, axis=0, keepdims=True)
                total = jnp.sum(totals * jnp.exp2(tops - top), axis=0, keepdims=True)
                index = g * GROUP + b
                lse = top + jnp.log2(total) - tnorm_ref[pl.ds(index, 1), :] * (LOG2E / (width * EPSILON))
                k = jnp.where(index < XN, places[0][0], places[-1][0])
                place = lax.rem(z + k, ZN) * XN + lax.rem(x + places[b % XN][1], XN)
                col_out[pl.ds(place, 1), :] = lse

            scan(0)
            for b in range(1, GROUP):
                scan(b)
                finish(b - 1)
            finish(GROUP - 1)
            return carry

        lax.fori_loop(0, u_ref.shape[0] // (GROUP * 128), blocks, 0)


def join(parts):
    top = jnp.max(parts, axis=0)
    return top + jnp.log2(jnp.sum(jnp.exp2(parts - top[None]), axis=0))


def row_pass(width, source, base, lse, chunk, places, group):
    rows, count = source.shape[0], len(places)
    first = lse is None
    inputs = [source, base] + ([] if first else [lse]) + chunk
    return pl.pallas_call(
        functools.partial(row_pass_kernel, width, places, first, group),
        out_shape=(
            pltpu.VMEM((count * 128, rows), jnp.float32),
            jax.ShapeDtypeStruct((count, 128), jnp.float32),
            jax.ShapeDtypeStruct((rows // 128, 128), jnp.float32),
        ),
        in_specs=[VMEM] * len(inputs), out_specs=(VMEM,) * 3,
        scratch_shapes=[pltpu.VMEM((count * 128, 2 * width), jnp.bfloat16), pltpu.VMEM((count * 128, 128), jnp.float32)],
        compiler_params=pltpu.CompilerParams(vmem_limit_bytes=ROW_VMEM),
        cost_estimate=pl.CostEstimate(flops=2 * 3 * rows * count * 128 * width, bytes_accessed=4 * rows * count * 128, transcendentals=rows * count * 128),
    )(*inputs)


def column_pass(width, parts, log_src, src_norm, tgt_norms, products, offsets):
    out = (sum(map(len, offsets)), 128)
    rows = log_src.size
    inputs = [*parts, log_src, src_norm, *tgt_norms, *products]
    size = rows * out[0] * 128
    return pl.pallas_call(
        functools.partial(column_pass_kernel, width, offsets),
        out_shape=(jax.ShapeDtypeStruct(log_src.shape, jnp.float32), jax.ShapeDtypeStruct(out, jnp.float32)),
        in_specs=[VMEM] * len(inputs), out_specs=(VMEM,) * 2,
        scratch_shapes=[pltpu.VMEM((8, rows), jnp.float32), pltpu.VMEM((GROUP * 128, 128), jnp.float32), pltpu.VMEM((GROUP * 128, 128), jnp.float32)],
        compiler_params=pltpu.CompilerParams(vmem_limit_bytes=4 * 2**20), name="column",
        cost_estimate=pl.CostEstimate(flops=8 * size, bytes_accessed=4 * size, transcendentals=size),
    )(*inputs)


def step(src_embed, tgt_embed, log_src, log_tgt, tgt_pot):
    width = src_embed.shape[1]
    rows = log_src.shape[0]
    log_src = log_src.reshape(-1, 128)
    base = (log_tgt + tgt_pot / EPSILON).reshape(-1, 128)

    plane = jnp.concatenate([tgt_embed] + [shift(tgt_embed, "x", XN, m) for m in (1, 3, 2)])
    around = (0, 1, 3, 2)
    half = plane.shape[0] // 2
    ups, downs = [plane], [plane]
    for _ in range(3):
        ups.append(shift(ups[-1], "z", ZN, 1))
        downs.append(shift(downs[-1], "z", ZN, -1))
    far = [shift(ups[3][:half], "z", ZN, 1), shift(downs[3][half:], "z", ZN, -1)]

    column = jnp.concatenate([src_embed] + [shift(src_embed, "y", YN, m) for m in (1, 2, 3)])
    other = shift(column, "c", CN, 1)
    source, src_norm = pl.pallas_call(
        functools.partial(pack_source_kernel, width),
        out_shape=(jax.ShapeDtypeStruct((rows, 2 * width), jnp.bfloat16), jax.ShapeDtypeStruct((rows // 128, 128), jnp.float32)),
        in_specs=[VMEM] * 2, out_specs=(VMEM,) * 2, compiler_params=pltpu.CompilerParams(vmem_limit_bytes=8 * 2**20), name="pack",
        cost_estimate=pl.CostEstimate(flops=2**23, bytes_accessed=2**23, transcendentals=0),
    )(column, other)

    chunks = [[plane], [ups[1], downs[1]], [ups[2], downs[2]], [ups[3], downs[3]], far]
    four = lambda k: [(k, m) for m in around]
    offsets = [four(0), four(1) + four(7), four(2) + four(6), four(3) + four(5), four(4)]
    lse, products, norms = None, [], []
    for index, (chunk, places) in enumerate(zip(chunks, offsets)):
        u, tnorm, lse = row_pass(width, source, base, lse, chunk, places, 2 if index in (1, 2) else 4)
        norms.append(tnorm)
        products.append(u)

    lse = join(jnp.stack([lse, shift(lse, "c", CN, 1)]))
    parts = [lse] + [shift(lse, "y", YN, m) for m in (1, 3, 2)]
    src_dual, column_lse = column_pass(width, parts, log_src, src_norm, norms, products, offsets)
    along_x = join(jnp.stack([column_lse] + [shift(column_lse, "x", XN, m) for m in (1, 3, 2)]))
    spread = jnp.broadcast_to(along_x[None], (ZN,) + along_x.shape)
    total = join(lax.all_to_all(spread, "z", 0, 0, tiled=True))
    return src_dual.reshape(-1), (-EPSILON * LN2 * total).reshape(-1)


def solution(mesh):
    torus = Mesh(mesh.devices.reshape(ZN, XN, YN, CN), ("z", "x", "y", "c"))
    src, tgt = ("z", "x"), ("y", "c")
    in_specs = (P(src + tgt, None), P(tgt + src, None), P(src), P(tgt), P(tgt))
    return jax.shard_map(step, mesh=torus, in_specs=in_specs, out_specs=(P(src), P(tgt)), check_vma=False)
```

profile of v0, /device:TPU:26, one launch (start us, length us, event | category | flops | bytes accessed | tf_op | source)
XLA Modules:
  0.0 111.4 jit_solution(12240527144504031785)
XLA Ops:
  0.6 1.6 %collective-permute-start.5 = (f32[128,256]{1,0:T(8,128)}, f32[128,256]{1,0:T(8,128)S(1)}, u32[]{:S(2)}, u32[]{:S(2)}) collective-permute-start(f32[128,256]{1,0:T(8,128)} %param.6), channel_id=1, source_target_pairs={{0,8},{8,16},{16,24},{24,0},{1,9},{9,17},{17,25},{25,1},{2,10},{10... | collective-permute-start | bytes 393224 | tf_op jit(solution)/shard_map/ppermute | solution.py:24
  2.2 0.5 collective-permute-start.4
  2.7 2.1 %collective-permute-start.6 = (f32[128,256]{1,0:T(8,128)}, f32[128,256]{1,0:T(8,128)S(1)}, u32[]{:S(2)}, u32[]{:S(2)}) collective-permute-start(f32[128,256]{1,0:T(8,128)} %param.6), channel_id=1, source_target_pairs={{0,16},{8,24},{16,0},{24,8},{1,17},{9,25},{17,1},{25,9},{2,18},{10... | collective-permute-start | bytes 393224 | tf_op jit(solution)/shard_map/ppermute | solution.py:24
  4.9 1.2 %collective-permute-start.1 = (f32[256,256]{1,0:T(8,128)}, f32[256,256]{1,0:T(8,128)S(1)}, u32[]{:S(2)}, u32[]{:S(2)}) collective-permute-start(f32[256,256]{1,0:T(8,128)} %param.5), channel_id=1, source_target_pairs={{0,4},{2,6},{4,0},{6,2},{1,5},{3,7},{5,1},{7,3},{8,12},{10,14},{12... | collective-permute-start | bytes 786440 | tf_op jit(solution)/shard_map/ppermute | solution.py:24
  6.1 0.0 collective-permute-start
  6.1 1.0 constant_dynamic-update-slice_fusion.3
  7.1 0.9 constant_dynamic-update-slice_fusion.7
  8.1 0.1 collective-permute-done.4
  8.2 3.2 %collective-permute-start.2 = (f32[256,256]{1,0:T(8,128)}, f32[256,256]{1,0:T(8,128)S(1)}, u32[]{:S(2)}, u32[]{:S(2)}) collective-permute-start(f32[256,256]{1,0:T(8,128)} %param.5), channel_id=1, source_target_pairs={{0,2},{2,4},{4,6},{6,0},{1,3},{3,5},{5,7},{7,1},{8,10},{10,12},{12... | collective-permute-start | bytes 786440 | tf_op jit(solution)/shard_map/ppermute | solution.py:24
  11.4 0.0 collective-permute-done.5
  11.4 0.0 collective-permute-done.6
  11.4 2.0 %collective-permute-start.8 = (f32[512,256]{1,0:T(8,128)S(1)}, f32[512,256]{1,0:T(8,128)S(1)}, u32[]{:S(2)}, u32[]{:S(2)}) collective-permute-start(f32[512,256]{1,0:T(8,128)S(1)} %constant_dynamic-update-slice_fusion.4.refs_2_), channel_id=1, source_target_pairs={{0,32},{32,64},{64,96},{96,128},{128,160},{160,192},{192,224},{224... | collective-permute-start | bytes 1572872 | tf_op jit(solution)/shard_map/ppermute | solution.py:24
  13.4 4.0 %collective-permute-start.7 = (f32[512,256]{1,0:T(8,128)S(1)}, f32[512,256]{1,0:T(8,128)S(1)}, u32[]{:S(2)}, u32[]{:S(2)}) collective-permute-start(f32[512,256]{1,0:T(8,128)S(1)} %constant_dynamic-update-slice_fusion.4.refs_2_), channel_id=1, source_target_pairs={{0,224},{32,0},{64,32},{96,64},{128,96},{160,128},{192,160},{224,1... | collective-permute-start | bytes 1572872 | tf_op jit(solution)/shard_map/ppermute | solution.py:24
  17.4 2.0 %collective-permute-done = f32[256,256]{1,0:T(8,128)S(1)} collective-permute-done((f32[256,256]{1,0:T(8,128)}, f32[256,256]{1,0:T(8,128)S(1)}, u32[]{:S(2)}, u32[]{:S(2)}) %collective-permute-start) | collective-permute-done | bytes 262176 | tf_op jit(solution)/shard_map/ppermute | solution.py:24
  19.5 0.0 collective-permute-done.2
  19.5 0.1 collective-permute-start.3
  19.6 8.0 %collective-permute-done.8.refs_4_ = f32[512,256]{1,0:T(8,128)S(1)} collective-permute-done((f32[512,256]{1,0:T(8,128)S(1)}, f32[512,256]{1,0:T(8,128)S(1)}, u32[]{:S(2)}, u32[]{:S(2)}) %collective-permute-start.8) | collective-permute-done | bytes 524320 | tf_op jit(solution)/shard_map/ppermute | solution.py:24
  27.6 0.0 collective-permute-done.7.refs_3_
  27.6 3.2 %collective-permute-start.9 = (f32[512,256]{1,0:T(8,128)S(1)}, f32[512,256]{1,0:T(8,128)S(1)}, u32[]{:S(2)}, u32[]{:S(2)}) collective-permute-start(f32[512,256]{1,0:T(8,128)S(1)} %collective-permute-done.7.refs_3_), channel_id=1, source_target_pairs={{0,224},{32,0},{64,32},{96,64},{128,96},{160,128},{192,160},{224,1... | collective-permute-start | bytes 1572872 | tf_op jit(solution)/shard_map/ppermute | solution.py:24
  30.8 0.7 add_bitcast_fusion.refs_1_
  31.6 8.6 %collective-permute-done.10.refs_4_ = f32[512,256]{1,0:T(8,128)S(1)} collective-permute-done((f32[512,256]{1,0:T(8,128)S(1)}, f32[512,256]{1,0:T(8,128)S(1)}, u32[]{:S(2)}, u32[]{:S(2)}) %collective-permute-start.10) | collective-permute-done | bytes 524320 | tf_op jit(solution)/shard_map/ppermute | solution.py:24
  40.2 3.2 %collective-permute-start.11 = (f32[512,256]{1,0:T(8,128)S(1)}, f32[512,256]{1,0:T(8,128)S(1)}, u32[]{:S(2)}, u32[]{:S(2)}) collective-permute-start(f32[512,256]{1,0:T(8,128)S(1)} %collective-permute-done.9.refs_3_), channel_id=1, source_target_pairs={{0,224},{32,0},{64,32},{96,64},{128,96},{160,128},{192,160},{224,1... | collective-permute-start | bytes 1572872 | tf_op jit(solution)/shard_map/ppermute | solution.py:24
  43.5 0.8 pack.1
  44.3 2.4 %shard_map.68 = (f32[512,2048]{1,0:T(8,128)S(1)}, f32[4,128]{1,0:T(4,128)S(1)}, f32[16,128]{1,0:T(8,128)S(1)}) custom-call(bf16[2048,512]{1,0:T(8,128)(2,1)S(1)} %get-tuple-element.21.refs_0_, f32[32,128]{1,0:T(8,128)S(1)} %add_bitcast_fusion.refs_1_, f32[512,256]{1,0:T(8,128)S(1)} %constant_dynamic-update-slice_fusion.4.refs_2_), custom_call_target="tpu_custom_call" | custom-call | flops 1610612736 | bytes 4194304 | tf_op jit(solution)/shard_map/pallas_call | solution.py:181
  46.7 6.5 %shard_map.69 = (f32[1024,2048]{1,0:T(8,128)S(1)}, f32[8,128]{1,0:T(8,128)S(1)}, f32[16,128]{1,0:T(8,128)S(1)}) custom-call(bf16[2048,512]{1,0:T(8,128)(2,1)S(1)} %get-tuple-element.21.refs_0_, f32[32,128]{1,0:T(8,128)S(1)} %add_bitcast_fusion.refs_1_, f32[16,128]{1,0:T(8,128)S(1)} %get-tuple-element.22.refs_2_, ...), custom_call_target="tpu_custom_call" | custom-call | flops 3221225472 | bytes 8388608 | tf_op jit(solution)/shard_map/pallas_call | solution.py:181
  53.2 6.5 %shard_map.70 = (f32[1024,2048]{1,0:T(8,128)S(1)}, f32[8,128]{1,0:T(8,128)S(1)}, f32[16,128]{1,0:T(8,128)S(1)}) custom-call(bf16[2048,512]{1,0:T(8,128)(2,1)S(1)} %get-tuple-element.21.refs_0_, f32[32,128]{1,0:T(8,128)S(1)} %add_bitcast_fusion.refs_1_, f32[16,128]{1,0:T(8,128)S(1)} %get-tuple-element.23.refs_2_, ...), custom_call_target="tpu_custom_call" | custom-call | flops 3221225472 | bytes 8388608 | tf_op jit(solution)/shard_map/pallas_call | solution.py:181
  59.6 0.0 collective-permute-done.12.refs_4_
  59.7 0.1 collective-permute-start.14
  59.8 0.0 collective-permute-done.11.refs_3_
  59.8 3.5 %collective-permute-start.13 = (f32[256,256]{1,0:T(8,128)S(1)}, f32[256,256]{1,0:T(8,128)S(1)}, u32[]{:S(2)}, u32[]{:S(2)}) collective-permute-start(f32[256,256]{1,0:T(8,128)S(1)} %slice.8), channel_id=1, source_target_pairs={{0,224},{32,0},{64,32},{96,64},{128,96},{160,128},{192,160},{224,1... | collective-permute-start | bytes 786440 | tf_op jit(solution)/shard_map/ppermute | solution.py:24
  63.3 4.7 %shard_map.71 = (f32[1024,2048]{1,0:T(8,128)S(1)}, f32[8,128]{1,0:T(8,128)S(1)}, f32[16,128]{1,0:T(8,128)S(1)}) custom-call(bf16[2048,512]{1,0:T(8,128)(2,1)S(1)} %get-tuple-element.21.refs_0_, f32[32,128]{1,0:T(8,128)S(1)} %add_bitcast_fusion.refs_1_, f32[16,128]{1,0:T(8,128)S(1)} %get-tuple-element.24.refs_2_, ...), custom_call_target="tpu_custom_call" | custom-call | flops 3221225472 | bytes 8388608 | tf_op jit(solution)/shard_map/pallas_call | solution.py:181
  68.1 2.5 %shard_map.72 = (f32[512,2048]{1,0:T(8,128)S(1)}, f32[4,128]{1,0:T(4,128)S(1)}, f32[16,128]{1,0:T(8,128)S(1)}) custom-call(bf16[2048,512]{1,0:T(8,128)(2,1)S(1)} %get-tuple-element.21.refs_0_, f32[32,128]{1,0:T(8,128)S(1)} %add_bitcast_fusion.refs_1_, f32[16,128]{1,0:T(8,128)S(1)} %get-tuple-element.25.refs_2_, ...), custom_call_target="tpu_custom_call" | custom-call | flops 1610612736 | bytes 4194304 | tf_op jit(solution)/shard_map/pallas_call | solution.py:181
  70.5 0.1 collective-permute-start.15
  70.6 1.2 %collective-permute-done.15 = f32[16,128]{1,0:T(8,128)S(1)} collective-permute-done((f32[16,128]{1,0:T(8,128)S(1)}, f32[16,128]{1,0:T(8,128)S(1)}, u32[]{:S(2)}, u32[]{:S(2)}) %collective-permute-start.15) | collective-permute-done | bytes 8224 | tf_op jit(solution)/shard_map/ppermute | solution.py:24
  71.8 1.2 %collective-permute-start.18 = (f32[16,128]{1,0:T(8,128)S(1)}, f32[16,128]{1,0:T(8,128)S(1)}, u32[]{:S(2)}, u32[]{:S(2)}) collective-permute-start(f32[16,128]{1,0:T(8,128)S(1)} %multiply_add_fusion.1.refs_0_), channel_id=1, source_target_pairs={{0,4},{2,6},{4,0},{6,2},{1,5},{3,7},{5,1},{7,3},{8,12},{10,14},{12... | collective-permute-start | bytes 24584 | tf_op jit(solution)/shard_map/ppermute | solution.py:24
  73.0 2.2 %collective-permute-start.17 = (f32[16,128]{1,0:T(8,128)S(1)}, f32[16,128]{1,0:T(8,128)S(1)}, u32[]{:S(2)}, u32[]{:S(2)}) collective-permute-start(f32[16,128]{1,0:T(8,128)S(1)} %multiply_add_fusion.1.refs_0_), channel_id=1, source_target_pairs={{0,2},{2,4},{4,6},{6,0},{1,3},{3,5},{5,7},{7,1},{8,10},{10,12},{12... | collective-permute-start | bytes 24584 | tf_op jit(solution)/shard_map/ppermute | solution.py:24
  75.3 0.0 collective-permute-start.16
  75.3 1.8 %collective-permute-done.18.refs_3_ = f32[16,128]{1,0:T(8,128)S(1)} collective-permute-done((f32[16,128]{1,0:T(8,128)S(1)}, f32[16,128]{1,0:T(8,128)S(1)}, u32[]{:S(2)}, u32[]{:S(2)}) %collective-permute-start.18) | collective-permute-done | bytes 8224 | tf_op jit(solution)/shard_map/ppermute | solution.py:24
  77.1 0.0 collective-permute-done.17.refs_2_
  77.1 3.0 %collective-permute-done.16.refs_1_ = f32[16,128]{1,0:T(8,128)S(1)} collective-permute-done((f32[16,128]{1,0:T(8,128)S(1)}, f32[16,128]{1,0:T(8,128)S(1)}, u32[]{:S(2)}, u32[]{:S(2)}) %collective-permute-start.16) | collective-permute-done | bytes 8224 | tf_op jit(solution)/shard_map/ppermute | solution.py:24
  80.1 8.4 %column.1 = (f32[16,128]{1,0:T(8,128)}, f32[32,128]{1,0:T(8,128)S(1)}) custom-call(f32[16,128]{1,0:T(8,128)S(1)} %multiply_add_fusion.1.refs_0_, f32[16,128]{1,0:T(8,128)S(1)} %collective-permute-done.16.refs_1_, f32[16,128]{1,0:T(8,128)S(1)} %collective-permute-done.17.refs_2_, f32[16,128]{1,0:T(8,128)S(1)} %collective-permute-done.18.refs_3_, ...), custom_call_target="tpu_custom_call" | custom-call | flops 67108864 | bytes 33554432 | tf_op jit(solution)/shard_map/column/pallas_call | solution.py:200
  88.5 1.5 %collective-permute-start.21 = (f32[32,128]{1,0:T(8,128)S(1)}, f32[32,128]{1,0:T(8,128)S(1)}, u32[]{:S(2)}, u32[]{:S(2)}) collective-permute-start(f32[32,128]{1,0:T(8,128)S(1)} %get-tuple-element.39), channel_id=1, source_target_pairs={{0,16},{8,24},{16,0},{24,8},{1,17},{9,25},{17,1},{25,9},{2,18},{10... | collective-permute-start | bytes 49160 | tf_op jit(solution)/shard_map/ppermute | solution.py:24
  90.0 2.7 %collective-permute-start.20 = (f32[32,128]{1,0:T(8,128)S(1)}, f32[32,128]{1,0:T(8,128)S(1)}, u32[]{:S(2)}, u32[]{:S(2)}) collective-permute-start(f32[32,128]{1,0:T(8,128)S(1)} %get-tuple-element.39), channel_id=1, source_target_pairs={{0,8},{8,16},{16,24},{24,0},{1,9},{9,17},{17,25},{25,1},{2,10},{10... | collective-permute-start | bytes 49160 | tf_op jit(solution)/shard_map/ppermute | solution.py:24
  92.6 1.2 %collective-permute-done.21 = f32[32,128]{1,0:T(8,128)S(1)} collective-permute-done((f32[32,128]{1,0:T(8,128)S(1)}, f32[32,128]{1,0:T(8,128)S(1)}, u32[]{:S(2)}, u32[]{:S(2)}) %collective-permute-start.21) | collective-permute-done | bytes 16416 | tf_op jit(solution)/shard_map/ppermute | solution.py:24
  93.8 0.2 collective-permute-done.20
  94.1 2.3 %collective-permute-done.19 = f32[32,128]{1,0:T(8,128)S(1)} collective-permute-done((f32[32,128]{1,0:T(8,128)S(1)}, f32[32,128]{1,0:T(8,128)S(1)}, u32[]{:S(2)}, u32[]{:S(2)}) %collective-permute-start.19) | collective-permute-done | bytes 16416 | tf_op jit(solution)/shard_map/ppermute | solution.py:24
  96.4 14.3 %all_to_all.5 = f32[8,32,128]{2,1,0:T(8,128)S(1)} all-to-all(f32[8,32,128]{2,1,0:T(8,128)S(1)} %broadcast_in_dim.2), channel_id=1, replica_groups=mesh['z'=8,'x'=4,'y'=4,'c'=2] {'z'}, dimensions={0} | all-to-all | bytes 262144 | tf_op jit(solution)/shard_map/all_to_all | solution.py:248
  110.8 0.6 multiply_bitcast_fusion
  (27 shorter events, 0.3 us)
Async XLA Ops:
  0.6 10.7 %collective-permute-start.5 = (f32[128,256]{1,0:T(8,128)}, f32[128,256]{1,0:T(8,128)S(1)}, u32[]{:S(2)}, u32[]{:S(2)}) collective-permute-start(f32[128,256]{1,0:T(8,128)} %param.6), channel_id=1, source_target_pairs={{0,8},{8,16},{16,24},{24,0},{1,9},{9,17},{17,25},{25,1},{2,10},{10... | collective-permute-start | bytes 393224 | tf_op jit(solution)/shard_map/ppermute | solution.py:24
  2.2 6.0 %collective-permute-start.4 = (f32[128,256]{1,0:T(8,128)}, f32[128,256]{1,0:T(8,128)S(1)}, u32[]{:S(2)}, u32[]{:S(2)}) collective-permute-start(f32[128,256]{1,0:T(8,128)} %param.6), channel_id=1, source_target_pairs={{0,24},{8,0},{16,8},{24,16},{1,25},{9,1},{17,9},{25,17},{2,26},{10... | collective-permute-start | bytes 393224 | tf_op jit(solution)/shard_map/ppermute | solution.py:24
  2.7 8.7 %collective-permute-start.6 = (f32[128,256]{1,0:T(8,128)}, f32[128,256]{1,0:T(8,128)S(1)}, u32[]{:S(2)}, u32[]{:S(2)}) collective-permute-start(f32[128,256]{1,0:T(8,128)} %param.6), channel_id=1, source_target_pairs={{0,16},{8,24},{16,0},{24,8},{1,17},{9,25},{17,1},{25,9},{2,18},{10... | collective-permute-start | bytes 393224 | tf_op jit(solution)/shard_map/ppermute | solution.py:24
  4.9 14.6 %collective-permute-start.1 = (f32[256,256]{1,0:T(8,128)}, f32[256,256]{1,0:T(8,128)S(1)}, u32[]{:S(2)}, u32[]{:S(2)}) collective-permute-start(f32[256,256]{1,0:T(8,128)} %param.5), channel_id=1, source_target_pairs={{0,4},{2,6},{4,0},{6,2},{1,5},{3,7},{5,1},{7,3},{8,12},{10,14},{12... | collective-permute-start | bytes 786440 | tf_op jit(solution)/shard_map/ppermute | solution.py:24
  6.1 13.3 %collective-permute-start = (f32[256,256]{1,0:T(8,128)}, f32[256,256]{1,0:T(8,128)S(1)}, u32[]{:S(2)}, u32[]{:S(2)}) collective-permute-start(f32[256,256]{1,0:T(8,128)} %param.5), channel_id=1, source_target_pairs={{0,6},{2,0},{4,2},{6,4},{1,7},{3,1},{5,3},{7,5},{8,14},{10,8},{12,... | collective-permute-start | bytes 786440 | tf_op jit(solution)/shard_map/ppermute | solution.py:24
  8.2 11.3 %collective-permute-start.2 = (f32[256,256]{1,0:T(8,128)}, f32[256,256]{1,0:T(8,128)S(1)}, u32[]{:S(2)}, u32[]{:S(2)}) collective-permute-start(f32[256,256]{1,0:T(8,128)} %param.5), channel_id=1, source_target_pairs={{0,2},{2,4},{4,6},{6,0},{1,3},{3,5},{5,7},{7,1},{8,10},{10,12},{12... | collective-permute-start | bytes 786440 | tf_op jit(solution)/shard_map/ppermute | solution.py:24
  11.4 16.2 %collective-permute-start.8 = (f32[512,256]{1,0:T(8,128)S(1)}, f32[512,256]{1,0:T(8,128)S(1)}, u32[]{:S(2)}, u32[]{:S(2)}) collective-permute-start(f32[512,256]{1,0:T(8,128)S(1)} %constant_dynamic-update-slice_fusion.4.refs_2_), channel_id=1, source_target_pairs={{0,32},{32,64},{64,96},{96,128},{128,160},{160,192},{192,224},{224... | collective-permute-start | bytes 1572872 | tf_op jit(solution)/shard_map/ppermute | solution.py:24
  13.4 14.2 %collective-permute-start.7 = (f32[512,256]{1,0:T(8,128)S(1)}, f32[512,256]{1,0:T(8,128)S(1)}, u32[]{:S(2)}, u32[]{:S(2)}) collective-permute-start(f32[512,256]{1,0:T(8,128)S(1)} %constant_dynamic-update-slice_fusion.4.refs_2_), channel_id=1, source_target_pairs={{0,224},{32,0},{64,32},{96,64},{128,96},{160,128},{192,160},{224,1... | collective-permute-start | bytes 1572872 | tf_op jit(solution)/shard_map/ppermute | solution.py:24
  19.5 24.0 %collective-permute-start.3 = (f32[1024,256]{1,0:T(8,128)S(1)}, f32[1024,256]{1,0:T(8,128)S(1)}, u32[]{:S(2)}, u32[]{:S(2)}) collective-permute-start(f32[1024,256]{1,0:T(8,128)S(1)} %constant_dynamic-update-slice_fusion.own_ref), channel_id=1, source_target_pairs={{0,1},{1,0},{2,3},{3,2},{4,5},{5,4},{6,7},{7,6},{8,9},{9,8},{10,11... | collective-permute-start | bytes 3145736 | tf_op jit(solution)/shard_map/ppermute | solution.py:24
  27.6 12.6 %collective-permute-start.10 = (f32[512,256]{1,0:T(8,128)S(1)}, f32[512,256]{1,0:T(8,128)S(1)}, u32[]{:S(2)}, u32[]{:S(2)}) collective-permute-start(f32[512,256]{1,0:T(8,128)S(1)} %collective-permute-done.8.refs_4_), channel_id=1, source_target_pairs={{0,32},{32,64},{64,96},{96,128},{128,160},{160,192},{192,224},{224... | collective-permute-start | bytes 1572872 | tf_op jit(solution)/shard_map/ppermute | solution.py:24
  27.6 12.6 %collective-permute-start.9 = (f32[512,256]{1,0:T(8,128)S(1)}, f32[512,256]{1,0:T(8,128)S(1)}, u32[]{:S(2)}, u32[]{:S(2)}) collective-permute-start(f32[512,256]{1,0:T(8,128)S(1)} %collective-permute-done.7.refs_3_), channel_id=1, source_target_pairs={{0,224},{32,0},{64,32},{96,64},{128,96},{160,128},{192,160},{224,1... | collective-permute-start | bytes 1572872 | tf_op jit(solution)/shard_map/ppermute | solution.py:24
  40.2 19.4 %collective-permute-start.12 = (f32[512,256]{1,0:T(8,128)S(1)}, f32[512,256]{1,0:T(8,128)S(1)}, u32[]{:S(2)}, u32[]{:S(2)}) collective-permute-start(f32[512,256]{1,0:T(8,128)S(1)} %collective-permute-done.10.refs_4_), channel_id=1, source_target_pairs={{0,32},{32,64},{64,96},{96,128},{128,160},{160,192},{192,224},{224... | collective-permute-start | bytes 1572872 | tf_op jit(solution)/shard_map/ppermute | solution.py:24
  40.2 19.6 %collective-permute-start.11 = (f32[512,256]{1,0:T(8,128)S(1)}, f32[512,256]{1,0:T(8,128)S(1)}, u32[]{:S(2)}, u32[]{:S(2)}) collective-permute-start(f32[512,256]{1,0:T(8,128)S(1)} %collective-permute-done.9.refs_3_), channel_id=1, source_target_pairs={{0,224},{32,0},{64,32},{96,64},{128,96},{160,128},{192,160},{224,1... | collective-permute-start | bytes 1572872 | tf_op jit(solution)/shard_map/ppermute | solution.py:24
  59.7 8.4 %collective-permute-start.14 = (f32[256,256]{1,0:T(8,128)S(1)}, f32[256,256]{1,0:T(8,128)S(1)}, u32[]{:S(2)}, u32[]{:S(2)}) collective-permute-start(f32[256,256]{1,0:T(8,128)S(1)} %slice.9), channel_id=1, source_target_pairs={{0,32},{32,64},{64,96},{96,128},{128,160},{160,192},{192,224},{224... | collective-permute-start | bytes 786440 | tf_op jit(solution)/shard_map/ppermute | solution.py:24
  59.8 8.3 %collective-permute-start.13 = (f32[256,256]{1,0:T(8,128)S(1)}, f32[256,256]{1,0:T(8,128)S(1)}, u32[]{:S(2)}, u32[]{:S(2)}) collective-permute-start(f32[256,256]{1,0:T(8,128)S(1)} %slice.8), channel_id=1, source_target_pairs={{0,224},{32,0},{64,32},{96,64},{128,96},{160,128},{192,160},{224,1... | collective-permute-start | bytes 786440 | tf_op jit(solution)/shard_map/ppermute | solution.py:24
  63.3 16.8 %copy-start = (f32[2048]{0:T(1024)S(1)}, f32[2048]{0:T(1024)}, u32[]{:S(2)}) copy-start(f32[2048]{0:T(1024)} %param.7) | copy-start | bytes 24580
  70.5 1.3 %collective-permute-start.15 = (f32[16,128]{1,0:T(8,128)S(1)}, f32[16,128]{1,0:T(8,128)S(1)}, u32[]{:S(2)}, u32[]{:S(2)}) collective-permute-start(f32[16,128]{1,0:T(8,128)S(1)} %get-tuple-element.26), channel_id=1, source_target_pairs={{0,1},{1,0},{2,3},{3,2},{4,5},{5,4},{6,7},{7,6},{8,9},{9,8},{10,11... | collective-permute-start | bytes 24584 | tf_op jit(solution)/shard_map/ppermute | solution.py:24
  71.8 5.2 %collective-permute-start.18 = (f32[16,128]{1,0:T(8,128)S(1)}, f32[16,128]{1,0:T(8,128)S(1)}, u32[]{:S(2)}, u32[]{:S(2)}) collective-permute-start(f32[16,128]{1,0:T(8,128)S(1)} %multiply_add_fusion.1.refs_0_), channel_id=1, source_target_pairs={{0,4},{2,6},{4,0},{6,2},{1,5},{3,7},{5,1},{7,3},{8,12},{10,14},{12... | collective-permute-start | bytes 24584 | tf_op jit(solution)/shard_map/ppermute | solution.py:24
  73.0 4.1 %collective-permute-start.17 = (f32[16,128]{1,0:T(8,128)S(1)}, f32[16,128]{1,0:T(8,128)S(1)}, u32[]{:S(2)}, u32[]{:S(2)}) collective-permute-start(f32[16,128]{1,0:T(8,128)S(1)} %multiply_add_fusion.1.refs_0_), channel_id=1, source_target_pairs={{0,2},{2,4},{4,6},{6,0},{1,3},{3,5},{5,7},{7,1},{8,10},{10,12},{12... | collective-permute-start | bytes 24584 | tf_op jit(solution)/shard_map/ppermute | solution.py:24
  75.3 4.9 %collective-permute-start.16 = (f32[16,128]{1,0:T(8,128)S(1)}, f32[16,128]{1,0:T(8,128)S(1)}, u32[]{:S(2)}, u32[]{:S(2)}) collective-permute-start(f32[16,128]{1,0:T(8,128)S(1)} %multiply_add_fusion.1.refs_0_), channel_id=1, source_target_pairs={{0,6},{2,0},{4,2},{6,4},{1,7},{3,1},{5,3},{7,5},{8,14},{10,8},{12,... | collective-permute-start | bytes 24584 | tf_op jit(solution)/shard_map/ppermute | solution.py:24
  88.5 5.3 %collective-permute-start.21 = (f32[32,128]{1,0:T(8,128)S(1)}, f32[32,128]{1,0:T(8,128)S(1)}, u32[]{:S(2)}, u32[]{:S(2)}) collective-permute-start(f32[32,128]{1,0:T(8,128)S(1)} %get-tuple-element.39), channel_id=1, source_target_pairs={{0,16},{8,24},{16,0},{24,8},{1,17},{9,25},{17,1},{25,9},{2,18},{10... | collective-permute-start | bytes 49160 | tf_op jit(solution)/shard_map/ppermute | solution.py:24
  90.0 4.1 %collective-permute-start.20 = (f32[32,128]{1,0:T(8,128)S(1)}, f32[32,128]{1,0:T(8,128)S(1)}, u32[]{:S(2)}, u32[]{:S(2)}) collective-permute-start(f32[32,128]{1,0:T(8,128)S(1)} %get-tuple-element.39), channel_id=1, source_target_pairs={{0,8},{8,16},{16,24},{24,0},{1,9},{9,17},{17,25},{25,1},{2,10},{10... | collective-permute-start | bytes 49160 | tf_op jit(solution)/shard_map/ppermute | solution.py:24
  92.6 3.7 %collective-permute-start.19 = (f32[32,128]{1,0:T(8,128)S(1)}, f32[32,128]{1,0:T(8,128)S(1)}, u32[]{:S(2)}, u32[]{:S(2)}) collective-permute-start(f32[32,128]{1,0:T(8,128)S(1)} %get-tuple-element.39), channel_id=1, source_target_pairs={{0,24},{8,0},{16,8},{24,16},{1,25},{9,1},{17,9},{25,17},{2,26},{10... | collective-permute-start | bytes 49160 | tf_op jit(solution)/shard_map/ppermute | solution.py:24
where the time goes:
time: 112 us; the launch traced here: 111 us
  starting transfers between devices  32.5 us (29%)
  Pallas kernels  31.8 us (28%)
  waiting for transfers between devices  28.5 us (25%)
  blocking collectives  14.3 us (13%)
  local copies, waits for them, and re-layouts  2.09 us (2%)
  other arithmetic  1.47 us (1%)
    ppermute x22, starting transfers between devices, shift(): lax.ppermute(value, axis, [(i, (i - back) % size) for i in range(size)])  32.5 us
    ppermute x22, waiting for transfers between devices, shift(): lax.ppermute(value, axis, [(i, (i - back) % size) for i in range(size)])  28.5 us
    pallas_call x5, Pallas kernels, row_pass(): pl.pallas_call(functools.partial(row_pass_kernel, width, places, first, g...  22.6 us
    all_to_all x1, blocking collectives, step(): total = join(lax.all_to_all(spread, 'z', 0, 0, tiled=True))  14.3 us
    pallas_call x1, Pallas kernels, column_pass(): pl.pallas_call(functools.partial(column_pass_kernel, width, offsets), out...  8.38 us
  transfers between devices with their start and end apart: 22, of which 10 were waited for; matrix products, arithmetic and copies ran while one was open for 3% of the time, Pallas kernels for 19%

commit v1 on v0

--- a/solution.py
+++ b/solution.py
@@ -217,10 +217,12 @@
     around = (0, 1, 3, 2)
     half = plane.shape[0] // 2
     ups, downs = [plane], [plane]
-    for _ in range(3):
+    for _ in range(2):
         ups.append(shift(ups[-1], "z", ZN, 1))
         downs.append(shift(downs[-1], "z", ZN, -1))
-    far = [shift(ups[3][:half], "z", ZN, 1), shift(downs[3][half:], "z", ZN, -1)]
+    third_up = [shift(part, "z", ZN, 1) for part in (ups[2][:half], ups[2][half:])]
+    third_down = [shift(part, "z", ZN, -1) for part in (downs[2][:half], downs[2][half:])]
+    far = [shift(third_up[0], "z", ZN, 1), shift(third_down[1], "z", ZN, -1)]
 
     column = jnp.concatenate([src_embed] + [shift(src_embed, "y", YN, m) for m in (1, 2, 3)])
     other = shift(column, "c", CN, 1)
@@ -231,7 +233,7 @@
         cost_estimate=pl.CostEstimate(flops=2**23, bytes_accessed=2**23, transcendentals=0),
     )(column, other)
 
-    chunks = [[plane], [ups[1], downs[1]], [ups[2], downs[2]], [ups[3], downs[3]], far]
+    chunks = [[plane], [ups[1], downs[1]], [ups[2], downs[2]], third_up + third_down, far]
     four = lambda k: [(k, m) for m in around]
     offsets = [four(0), four(1) + four(7), four(2) + four(6), four(3) + four(5), four(4)]
     lse, products, norms = None, [], []

time: 112 us -> 115 us (1.027)
  starting transfers between devices: 32.5 us -> 35.4 us
    ppermute x22 -> x24, starting transfers between devices: 32.5 us -> 35.4 us  [shift(): lax.ppermute(value, axis, [(i, (i - back) % size) for i in range(size)])]
    ppermute x22 -> x24, waiting for transfers between devices: 28.5 us -> 28.9 us  [shift(): lax.ppermute(value, axis, [(i, (i - back) % size) for i in range(size)])]
  transfers between devices with their start and end apart: 22 -> 24, of which waited for: 10 -> 12; matrix products, arithmetic and copies ran while one was open for 3% -> 2% of each run, Pallas kernels for 19% -> 18%
where the time goes in v1:
time: 115 us
  starting transfers between devices  35.4 us (31%)
  Pallas kernels  31.7 us (28%)
  waiting for transfers between devices  28.9 us (25%)
  blocking collectives  14.3 us (12%)
  local copies, waits for them, and re-layouts  2.09 us (2%)
  other arithmetic  1.47 us (1%)
    ppermute x24, starting transfers between devices, shift(): lax.ppermute(value, axis, [(i, (i - back) % size) for i in range(size)])  35.4 us
    ppermute x24, waiting for transfers between devices, shift(): lax.ppermute(value, axis, [(i, (i - back) % size) for i in range(size)])  28.9 us
    pallas_call x5, Pallas kernels, row_pass(): pl.pallas_call(functools.partial(row_pass_kernel, width, places, first, g...  22.5 us
    all_to_all x1, blocking collectives, step(): total = join(lax.all_to_all(spread, 'z', 0, 0, tiled=True))  14.3 us
    pallas_call x1, Pallas kernels, column_pass(): pl.pallas_call(functools.partial(column_pass_kernel, width, offsets), out...  8.38 us
  transfers between devices with their start and end apart: 24, of which 12 were waited for; matrix products, arithmetic and copies ran while one was open for 2% of the time, Pallas kernels for 18%

profile of v1, /device:TPU:26, one launch (start us, length us, event | category | flops | bytes accessed | tf_op | source)
XLA Modules:
  0.0 114.6 jit_solution(3832031113038181935)
XLA Ops:
  0.6 0.6 collective-permute-start.4
  1.2 1.5 %collective-permute-start.5 = (f32[128,256]{1,0:T(8,128)}, f32[128,256]{1,0:T(8,128)S(1)}, u32[]{:S(2)}, u32[]{:S(2)}) collective-permute-start(f32[128,256]{1,0:T(8,128)} %param.6), channel_id=1, source_target_pairs={{0,8},{8,16},{16,24},{24,0},{1,9},{9,17},{17,25},{25,1},{2,10},{10... | collective-permute-start | bytes 393224 | tf_op jit(solution)/shard_map/ppermute | solution.py:24
  2.7 3.3 %collective-permute-start.6 = (f32[128,256]{1,0:T(8,128)}, f32[128,256]{1,0:T(8,128)S(1)}, u32[]{:S(2)}, u32[]{:S(2)}) collective-permute-start(f32[128,256]{1,0:T(8,128)} %param.6), channel_id=1, source_target_pairs={{0,16},{8,24},{16,0},{24,8},{1,17},{9,25},{17,1},{25,9},{2,18},{10... | collective-permute-start | bytes 393224 | tf_op jit(solution)/shard_map/ppermute | solution.py:24
  6.1 1.2 %collective-permute-start.1 = (f32[256,256]{1,0:T(8,128)}, f32[256,256]{1,0:T(8,128)S(1)}, u32[]{:S(2)}, u32[]{:S(2)}) collective-permute-start(f32[256,256]{1,0:T(8,128)} %param.5), channel_id=1, source_target_pairs={{0,4},{2,6},{4,0},{6,2},{1,5},{3,7},{5,1},{7,3},{8,12},{10,14},{12... | collective-permute-start | bytes 786440 | tf_op jit(solution)/shard_map/ppermute | solution.py:24
  7.3 0.0 collective-permute-start
  7.3 0.9 constant_dynamic-update-slice_fusion.7
  8.3 0.3 collective-permute-done.5
  8.6 1.3 %collective-permute-done.6 = f32[128,256]{1,0:T(8,128)S(1)} collective-permute-done((f32[128,256]{1,0:T(8,128)}, f32[128,256]{1,0:T(8,128)S(1)}, u32[]{:S(2)}, u32[]{:S(2)}) %collective-permute-start.6) | collective-permute-done | bytes 131104 | tf_op jit(solution)/shard_map/ppermute | solution.py:24
  9.9 2.0 %collective-permute-start.8 = (f32[512,256]{1,0:T(8,128)S(1)}, f32[512,256]{1,0:T(8,128)S(1)}, u32[]{:S(2)}, u32[]{:S(2)}) collective-permute-start(f32[512,256]{1,0:T(8,128)S(1)} %constant_dynamic-update-slice_fusion.4.refs_2_), channel_id=1, source_target_pairs={{0,32},{32,64},{64,96},{96,128},{128,160},{160,192},{192,224},{224... | collective-permute-start | bytes 1572872 | tf_op jit(solution)/shard_map/ppermute | solution.py:24
  11.9 1.6 %collective-permute-start.2 = (f32[256,256]{1,0:T(8,128)}, f32[256,256]{1,0:T(8,128)S(1)}, u32[]{:S(2)}, u32[]{:S(2)}) collective-permute-start(f32[256,256]{1,0:T(8,128)} %param.5), channel_id=1, source_target_pairs={{0,2},{2,4},{4,6},{6,0},{1,3},{3,5},{5,7},{7,1},{8,10},{10,12},{12... | collective-permute-start | bytes 786440 | tf_op jit(solution)/shard_map/ppermute | solution.py:24
  13.5 1.0 constant_dynamic-update-slice_fusion.3
  14.5 4.1 %collective-permute-start.7 = (f32[512,256]{1,0:T(8,128)S(1)}, f32[512,256]{1,0:T(8,128)S(1)}, u32[]{:S(2)}, u32[]{:S(2)}) collective-permute-start(f32[512,256]{1,0:T(8,128)S(1)} %constant_dynamic-update-slice_fusion.4.refs_2_), channel_id=1, source_target_pairs={{0,224},{32,0},{64,32},{96,64},{128,96},{160,128},{192,160},{224,1... | collective-permute-start | bytes 1572872 | tf_op jit(solution)/shard_map/ppermute | solution.py:24
  18.7 2.0 %collective-permute-done = f32[256,256]{1,0:T(8,128)S(1)} collective-permute-done((f32[256,256]{1,0:T(8,128)}, f32[256,256]{1,0:T(8,128)S(1)}, u32[]{:S(2)}, u32[]{:S(2)}) %collective-permute-start) | collective-permute-done | bytes 262176 | tf_op jit(solution)/shard_map/ppermute | solution.py:24
  20.6 0.0 collective-permute-done.1
  20.7 0.0 collective-permute-done.2
  20.7 0.1 collective-permute-start.3
  20.8 6.3 %collective-permute-done.8.refs_4_ = f32[512,256]{1,0:T(8,128)S(1)} collective-permute-done((f32[512,256]{1,0:T(8,128)S(1)}, f32[512,256]{1,0:T(8,128)S(1)}, u32[]{:S(2)}, u32[]{:S(2)}) %collective-permute-start.8) | collective-permute-done | bytes 524320 | tf_op jit(solution)/shard_map/ppermute | solution.py:24
  27.1 1.0 collective-permute-done.7.refs_3_
  28.2 3.7 %collective-permute-start.9 = (f32[512,256]{1,0:T(8,128)S(1)}, f32[512,256]{1,0:T(8,128)S(1)}, u32[]{:S(2)}, u32[]{:S(2)}) collective-permute-start(f32[512,256]{1,0:T(8,128)S(1)} %collective-permute-done.7.refs_3_), channel_id=1, source_target_pairs={{0,224},{32,0},{64,32},{96,64},{128,96},{160,128},{192,160},{224,1... | collective-permute-start | bytes 1572872 | tf_op jit(solution)/shard_map/ppermute | solution.py:24
  31.8 0.7 add_bitcast_fusion.refs_1_
  32.6 8.2 %collective-permute-done.10.refs_4_ = f32[512,256]{1,0:T(8,128)S(1)} collective-permute-done((f32[512,256]{1,0:T(8,128)S(1)}, f32[512,256]{1,0:T(8,128)S(1)}, u32[]{:S(2)}, u32[]{:S(2)}) %collective-permute-start.10) | collective-permute-done | bytes 524320 | tf_op jit(solution)/shard_map/ppermute | solution.py:24
  40.8 0.1 collective-permute-start.14
  40.9 0.1 collective-permute-start.13
  41.0 3.3 %collective-permute-start.12 = (f32[256,256]{1,0:T(8,128)S(1)}, f32[256,256]{1,0:T(8,128)S(1)}, u32[]{:S(2)}, u32[]{:S(2)}) collective-permute-start(f32[256,256]{1,0:T(8,128)S(1)} %get-tuple-element.42), channel_id=1, source_target_pairs={{0,224},{32,0},{64,32},{96,64},{128,96},{160,128},{192,160},{224,1... | collective-permute-start | bytes 786440 | tf_op jit(solution)/shard_map/ppermute | solution.py:24
  44.3 1.9 %collective-permute-start.11 = (f32[256,256]{1,0:T(8,128)S(1)}, f32[256,256]{1,0:T(8,128)S(1)}, u32[]{:S(2)}, u32[]{:S(2)}) collective-permute-start(f32[256,256]{1,0:T(8,128)S(1)} %get-tuple-element.43), channel_id=1, source_target_pairs={{0,224},{32,0},{64,32},{96,64},{128,96},{160,128},{192,160},{224,1... | collective-permute-start | bytes 786440 | tf_op jit(solution)/shard_map/ppermute | solution.py:24
  46.3 0.8 pack.1
  47.1 2.4 %shard_map.68 = (f32[512,2048]{1,0:T(8,128)S(1)}, f32[4,128]{1,0:T(4,128)S(1)}, f32[16,128]{1,0:T(8,128)S(1)}) custom-call(bf16[2048,512]{1,0:T(8,128)(2,1)S(1)} %get-tuple-element.21.refs_0_, f32[32,128]{1,0:T(8,128)S(1)} %add_bitcast_fusion.refs_1_, f32[512,256]{1,0:T(8,128)S(1)} %constant_dynamic-update-slice_fusion.4.refs_2_), custom_call_target="tpu_custom_call" | custom-call | flops 1610612736 | bytes 4194304 | tf_op jit(solution)/shard_map/pallas_call | solution.py:181
  49.5 6.5 %shard_map.69 = (f32[1024,2048]{1,0:T(8,128)S(1)}, f32[8,128]{1,0:T(8,128)S(1)}, f32[16,128]{1,0:T(8,128)S(1)}) custom-call(bf16[2048,512]{1,0:T(8,128)(2,1)S(1)} %get-tuple-element.21.refs_0_, f32[32,128]{1,0:T(8,128)S(1)} %add_bitcast_fusion.refs_1_, f32[16,128]{1,0:T(8,128)S(1)} %get-tuple-element.22.refs_2_, ...), custom_call_target="tpu_custom_call" | custom-call | flops 3221225472 | bytes 8388608 | tf_op jit(solution)/shard_map/pallas_call | solution.py:181
  56.0 6.5 %shard_map.70 = (f32[1024,2048]{1,0:T(8,128)S(1)}, f32[8,128]{1,0:T(8,128)S(1)}, f32[16,128]{1,0:T(8,128)S(1)}) custom-call(bf16[2048,512]{1,0:T(8,128)(2,1)S(1)} %get-tuple-element.21.refs_0_, f32[32,128]{1,0:T(8,128)S(1)} %add_bitcast_fusion.refs_1_, f32[16,128]{1,0:T(8,128)S(1)} %get-tuple-element.23.refs_2_, ...), custom_call_target="tpu_custom_call" | custom-call | flops 3221225472 | bytes 8388608 | tf_op jit(solution)/shard_map/pallas_call | solution.py:181
  62.4 0.2 collective-permute-start.16
  62.6 3.1 %collective-permute-start.15 = (f32[256,256]{1,0:T(8,128)S(1)}, f32[256,256]{1,0:T(8,128)S(1)}, u32[]{:S(2)}, u32[]{:S(2)}) collective-permute-start(f32[256,256]{1,0:T(8,128)S(1)} %collective-permute-done.11.refs_3_), channel_id=1, source_target_pairs={{0,224},{32,0},{64,32},{96,64},{128,96},{160,128},{192,160},{224,1... | collective-permute-start | bytes 786440 | tf_op jit(solution)/shard_map/ppermute | solution.py:24
  65.8 4.7 %shard_map.71 = (f32[1024,2048]{1,0:T(8,128)S(1)}, f32[8,128]{1,0:T(8,128)S(1)}, f32[16,128]{1,0:T(8,128)S(1)}) custom-call(bf16[2048,512]{1,0:T(8,128)(2,1)S(1)} %get-tuple-element.21.refs_0_, f32[32,128]{1,0:T(8,128)S(1)} %add_bitcast_fusion.refs_1_, f32[16,128]{1,0:T(8,128)S(1)} %get-tuple-element.24.refs_2_, ...), custom_call_target="tpu_custom_call" | custom-call | flops 3221225472 | bytes 8388608 | tf_op jit(solution)/shard_map/pallas_call | solution.py:181
  70.5 2.4 %shard_map.72 = (f32[512,2048]{1,0:T(8,128)S(1)}, f32[4,128]{1,0:T(4,128)S(1)}, f32[16,128]{1,0:T(8,128)S(1)}) custom-call(bf16[2048,512]{1,0:T(8,128)(2,1)S(1)} %get-tuple-element.21.refs_0_, f32[32,128]{1,0:T(8,128)S(1)} %add_bitcast_fusion.refs_1_, f32[16,128]{1,0:T(8,128)S(1)} %get-tuple-element.25.refs_2_, ...), custom_call_target="tpu_custom_call" | custom-call | flops 1610612736 | bytes 4194304 | tf_op jit(solution)/shard_map/pallas_call | solution.py:181
  72.9 0.1 collective-permute-start.17
  73.0 1.2 %collective-permute-done.17 = f32[16,128]{1,0:T(8,128)S(1)} collective-permute-done((f32[16,128]{1,0:T(8,128)S(1)}, f32[16,128]{1,0:T(8,128)S(1)}, u32[]{:S(2)}, u32[]{:S(2)}) %collective-permute-start.17) | collective-permute-done | bytes 8224 | tf_op jit(solution)/shard_map/ppermute | solution.py:24
  74.2 1.2 %collective-permute-start.20 = (f32[16,128]{1,0:T(8,128)S(1)}, f32[16,128]{1,0:T(8,128)S(1)}, u32[]{:S(2)}, u32[]{:S(2)}) collective-permute-start(f32[16,128]{1,0:T(8,128)S(1)} %multiply_add_fusion.1.refs_0_), channel_id=1, source_target_pairs={{0,4},{2,6},{4,0},{6,2},{1,5},{3,7},{5,1},{7,3},{8,12},{10,14},{12... | collective-permute-start | bytes 24584 | tf_op jit(solution)/shard_map/ppermute | solution.py:24
  75.4 2.3 %collective-permute-start.19 = (f32[16,128]{1,0:T(8,128)S(1)}, f32[16,128]{1,0:T(8,128)S(1)}, u32[]{:S(2)}, u32[]{:S(2)}) collective-permute-start(f32[16,128]{1,0:T(8,128)S(1)} %multiply_add_fusion.1.refs_0_), channel_id=1, source_target_pairs={{0,2},{2,4},{4,6},{6,0},{1,3},{3,5},{5,7},{7,1},{8,10},{10,12},{12... | collective-permute-start | bytes 24584 | tf_op jit(solution)/shard_map/ppermute | solution.py:24
  77.7 0.0 collective-permute-start.18
  77.7 1.7 %collective-permute-done.20.refs_3_ = f32[16,128]{1,0:T(8,128)S(1)} collective-permute-done((f32[16,128]{1,0:T(8,128)S(1)}, f32[16,128]{1,0:T(8,128)S(1)}, u32[]{:S(2)}, u32[]{:S(2)}) %collective-permute-start.20) | collective-permute-done | bytes 8224 | tf_op jit(solution)/shard_map/ppermute | solution.py:24
  79.5 3.1 %collective-permute-done.18.refs_1_ = f32[16,128]{1,0:T(8,128)S(1)} collective-permute-done((f32[16,128]{1,0:T(8,128)S(1)}, f32[16,128]{1,0:T(8,128)S(1)}, u32[]{:S(2)}, u32[]{:S(2)}) %collective-permute-start.18) | collective-permute-done | bytes 8224 | tf_op jit(solution)/shard_map/ppermute | solution.py:24
  82.6 8.4 %column.1 = (f32[16,128]{1,0:T(8,128)}, f32[32,128]{1,0:T(8,128)S(1)}) custom-call(f32[16,128]{1,0:T(8,128)S(1)} %multiply_add_fusion.1.refs_0_, f32[16,128]{1,0:T(8,128)S(1)} %collective-permute-done.18.refs_1_, f32[16,128]{1,0:T(8,128)S(1)} %collective-permute-done.19.refs_2_, f32[16,128]{1,0:T(8,128)S(1)} %collective-permute-done.20.refs_3_, ...), custom_call_target="tpu_custom_call" | custom-call | flops 67108864 | bytes 33554432 | tf_op jit(solution)/shard_map/column/pallas_call | solution.py:200
  91.0 0.8 collective-permute-start.23
  91.8 4.1 %collective-permute-start.22 = (f32[32,128]{1,0:T(8,128)S(1)}, f32[32,128]{1,0:T(8,128)S(1)}, u32[]{:S(2)}, u32[]{:S(2)}) collective-permute-start(f32[32,128]{1,0:T(8,128)S(1)} %get-tuple-element.39), channel_id=1, source_target_pairs={{0,8},{8,16},{16,24},{24,0},{1,9},{9,17},{17,25},{25,1},{2,10},{10... | collective-permute-start | bytes 49160 | tf_op jit(solution)/shard_map/ppermute | solution.py:24
  95.9 0.7 collective-permute-done.23
  96.5 0.8 collective-permute-done.22
  97.3 2.3 %collective-permute-done.21 = f32[32,128]{1,0:T(8,128)S(1)} collective-permute-done((f32[32,128]{1,0:T(8,128)S(1)}, f32[32,128]{1,0:T(8,128)S(1)}, u32[]{:S(2)}, u32[]{:S(2)}) %collective-permute-start.21) | collective-permute-done | bytes 16416 | tf_op jit(solution)/shard_map/ppermute | solution.py:24
  99.7 14.3 %all_to_all.5 = f32[8,32,128]{2,1,0:T(8,128)S(1)} all-to-all(f32[8,32,128]{2,1,0:T(8,128)S(1)} %broadcast_in_dim.2), channel_id=1, replica_groups=mesh['z'=8,'x'=4,'y'=4,'c'=2] {'z'}, dimensions={0} | all-to-all | bytes 262144 | tf_op jit(solution)/shard_map/all_to_all | solution.py:250
  114.0 0.6 multiply_bitcast_fusion
  (31 shorter events, 0.3 us)
Async XLA Ops:
  0.6 7.6 %collective-permute-start.4 = (f32[128,256]{1,0:T(8,128)}, f32[128,256]{1,0:T(8,128)S(1)}, u32[]{:S(2)}, u32[]{:S(2)}) collective-permute-start(f32[128,256]{1,0:T(8,128)} %param.6), channel_id=1, source_target_pairs={{0,24},{8,0},{16,8},{24,16},{1,25},{9,1},{17,9},{25,17},{2,26},{10... | collective-permute-start | bytes 393224 | tf_op jit(solution)/shard_map/ppermute | solution.py:24
  1.2 7.3 %collective-permute-start.5 = (f32[128,256]{1,0:T(8,128)}, f32[128,256]{1,0:T(8,128)S(1)}, u32[]{:S(2)}, u32[]{:S(2)}) collective-permute-start(f32[128,256]{1,0:T(8,128)} %param.6), channel_id=1, source_target_pairs={{0,8},{8,16},{16,24},{24,0},{1,9},{9,17},{17,25},{25,1},{2,10},{10... | collective-permute-start | bytes 393224 | tf_op jit(solution)/shard_map/ppermute | solution.py:24
  2.7 7.2 %collective-permute-start.6 = (f32[128,256]{1,0:T(8,128)}, f32[128,256]{1,0:T(8,128)S(1)}, u32[]{:S(2)}, u32[]{:S(2)}) collective-permute-start(f32[128,256]{1,0:T(8,128)} %param.6), channel_id=1, source_target_pairs={{0,16},{8,24},{16,0},{24,8},{1,17},{9,25},{17,1},{25,9},{2,18},{10... | collective-permute-start | bytes 393224 | tf_op jit(solution)/shard_map/ppermute | solution.py:24
  6.1 14.6 %collective-permute-start.1 = (f32[256,256]{1,0:T(8,128)}, f32[256,256]{1,0:T(8,128)S(1)}, u32[]{:S(2)}, u32[]{:S(2)}) collective-permute-start(f32[256,256]{1,0:T(8,128)} %param.5), channel_id=1, source_target_pairs={{0,4},{2,6},{4,0},{6,2},{1,5},{3,7},{5,1},{7,3},{8,12},{10,14},{12... | collective-permute-start | bytes 786440 | tf_op jit(solution)/shard_map/ppermute | solution.py:24
  7.3 13.3 %collective-permute-start = (f32[256,256]{1,0:T(8,128)}, f32[256,256]{1,0:T(8,128)S(1)}, u32[]{:S(2)}, u32[]{:S(2)}) collective-permute-start(f32[256,256]{1,0:T(8,128)} %param.5), channel_id=1, source_target_pairs={{0,6},{2,0},{4,2},{6,4},{1,7},{3,1},{5,3},{7,5},{8,14},{10,8},{12,... | collective-permute-start | bytes 786440 | tf_op jit(solution)/shard_map/ppermute | solution.py:24
  9.9 17.2 %collective-permute-start.8 = (f32[512,256]{1,0:T(8,128)S(1)}, f32[512,256]{1,0:T(8,128)S(1)}, u32[]{:S(2)}, u32[]{:S(2)}) collective-permute-start(f32[512,256]{1,0:T(8,128)S(1)} %constant_dynamic-update-slice_fusion.4.refs_2_), channel_id=1, source_target_pairs={{0,32},{32,64},{64,96},{96,128},{128,160},{160,192},{192,224},{224... | collective-permute-start | bytes 1572872 | tf_op jit(solution)/shard_map/ppermute | solution.py:24
  11.9 8.8 %collective-permute-start.2 = (f32[256,256]{1,0:T(8,128)}, f32[256,256]{1,0:T(8,128)S(1)}, u32[]{:S(2)}, u32[]{:S(2)}) collective-permute-start(f32[256,256]{1,0:T(8,128)} %param.5), channel_id=1, source_target_pairs={{0,2},{2,4},{4,6},{6,0},{1,3},{3,5},{5,7},{7,1},{8,10},{10,12},{12... | collective-permute-start | bytes 786440 | tf_op jit(solution)/shard_map/ppermute | solution.py:24
  14.5 13.6 %collective-permute-start.7 = (f32[512,256]{1,0:T(8,128)S(1)}, f32[512,256]{1,0:T(8,128)S(1)}, u32[]{:S(2)}, u32[]{:S(2)}) collective-permute-start(f32[512,256]{1,0:T(8,128)S(1)} %constant_dynamic-update-slice_fusion.4.refs_2_), channel_id=1, source_target_pairs={{0,224},{32,0},{64,32},{96,64},{128,96},{160,128},{192,160},{224,1... | collective-permute-start | bytes 1572872 | tf_op jit(solution)/shard_map/ppermute | solution.py:24
  20.7 25.6 %collective-permute-start.3 = (f32[1024,256]{1,0:T(8,128)S(1)}, f32[1024,256]{1,0:T(8,128)S(1)}, u32[]{:S(2)}, u32[]{:S(2)}) collective-permute-start(f32[1024,256]{1,0:T(8,128)S(1)} %constant_dynamic-update-slice_fusion.own_ref), channel_id=1, source_target_pairs={{0,1},{1,0},{2,3},{3,2},{4,5},{5,4},{6,7},{7,6},{8,9},{9,8},{10,11... | collective-permute-start | bytes 3145736 | tf_op jit(solution)/shard_map/ppermute | solution.py:24
  27.1 13.6 %collective-permute-start.10 = (f32[512,256]{1,0:T(8,128)S(1)}, f32[512,256]{1,0:T(8,128)S(1)}, u32[]{:S(2)}, u32[]{:S(2)}) collective-permute-start(f32[512,256]{1,0:T(8,128)S(1)} %collective-permute-done.8.refs_4_), channel_id=1, source_target_pairs={{0,32},{32,64},{64,96},{96,128},{128,160},{160,192},{192,224},{224... | collective-permute-start | bytes 1572872 | tf_op jit(solution)/shard_map/ppermute | solution.py:24
  28.2 12.8 %collective-permute-start.9 = (f32[512,256]{1,0:T(8,128)S(1)}, f32[512,256]{1,0:T(8,128)S(1)}, u32[]{:S(2)}, u32[]{:S(2)}) collective-permute-start(f32[512,256]{1,0:T(8,128)S(1)} %collective-permute-done.7.refs_3_), channel_id=1, source_target_pairs={{0,224},{32,0},{64,32},{96,64},{128,96},{160,128},{192,160},{224,1... | collective-permute-start | bytes 1572872 | tf_op jit(solution)/shard_map/ppermute | solution.py:24
  40.8 21.6 %collective-permute-start.14 = (f32[256,256]{1,0:T(8,128)S(1)}, f32[256,256]{1,0:T(8,128)S(1)}, u32[]{:S(2)}, u32[]{:S(2)}) collective-permute-start(f32[256,256]{1,0:T(8,128)S(1)} %get-tuple-element.40), channel_id=1, source_target_pairs={{0,32},{32,64},{64,96},{96,128},{128,160},{160,192},{192,224},{224... | collective-permute-start | bytes 786440 | tf_op jit(solution)/shard_map/ppermute | solution.py:24
  40.9 24.9 %collective-permute-start.13 = (f32[256,256]{1,0:T(8,128)S(1)}, f32[256,256]{1,0:T(8,128)S(1)}, u32[]{:S(2)}, u32[]{:S(2)}) collective-permute-start(f32[256,256]{1,0:T(8,128)S(1)} %get-tuple-element.41), channel_id=1, source_target_pairs={{0,32},{32,64},{64,96},{96,128},{128,160},{160,192},{192,224},{224... | collective-permute-start | bytes 786440 | tf_op jit(solution)/shard_map/ppermute | solution.py:24
  41.0 24.7 %collective-permute-start.12 = (f32[256,256]{1,0:T(8,128)S(1)}, f32[256,256]{1,0:T(8,128)S(1)}, u32[]{:S(2)}, u32[]{:S(2)}) collective-permute-start(f32[256,256]{1,0:T(8,128)S(1)} %get-tuple-element.42), channel_id=1, source_target_pairs={{0,224},{32,0},{64,32},{96,64},{128,96},{160,128},{192,160},{224,1... | collective-permute-start | bytes 786440 | tf_op jit(solution)/shard_map/ppermute | solution.py:24
  44.3 18.3 %collective-permute-start.11 = (f32[256,256]{1,0:T(8,128)S(1)}, f32[256,256]{1,0:T(8,128)S(1)}, u32[]{:S(2)}, u32[]{:S(2)}) collective-permute-start(f32[256,256]{1,0:T(8,128)S(1)} %get-tuple-element.43), channel_id=1, source_target_pairs={{0,224},{32,0},{64,32},{96,64},{128,96},{160,128},{192,160},{224,1... | collective-permute-start | bytes 786440 | tf_op jit(solution)/shard_map/ppermute | solution.py:24
  62.4 8.1 %collective-permute-start.16 = (f32[256,256]{1,0:T(8,128)S(1)}, f32[256,256]{1,0:T(8,128)S(1)}, u32[]{:S(2)}, u32[]{:S(2)}) collective-permute-start(f32[256,256]{1,0:T(8,128)S(1)} %collective-permute-done.14.refs_6_), channel_id=1, source_target_pairs={{0,32},{32,64},{64,96},{96,128},{128,160},{160,192},{192,224},{224... | collective-permute-start | bytes 786440 | tf_op jit(solution)/shard_map/ppermute | solution.py:24
  62.6 7.9 %collective-permute-start.15 = (f32[256,256]{1,0:T(8,128)S(1)}, f32[256,256]{1,0:T(8,128)S(1)}, u32[]{:S(2)}, u32[]{:S(2)}) collective-permute-start(f32[256,256]{1,0:T(8,128)S(1)} %collective-permute-done.11.refs_3_), channel_id=1, source_target_pairs={{0,224},{32,0},{64,32},{96,64},{128,96},{160,128},{192,160},{224,1... | collective-permute-start | bytes 786440 | tf_op jit(solution)/shard_map/ppermute | solution.py:24
  65.7 16.9 %copy-start = (f32[2048]{0:T(1024)S(1)}, f32[2048]{0:T(1024)}, u32[]{:S(2)}) copy-start(f32[2048]{0:T(1024)} %param.7) | copy-start | bytes 24580
  72.9 1.3 %collective-permute-start.17 = (f32[16,128]{1,0:T(8,128)S(1)}, f32[16,128]{1,0:T(8,128)S(1)}, u32[]{:S(2)}, u32[]{:S(2)}) collective-permute-start(f32[16,128]{1,0:T(8,128)S(1)} %get-tuple-element.26), channel_id=1, source_target_pairs={{0,1},{1,0},{2,3},{3,2},{4,5},{5,4},{6,7},{7,6},{8,9},{9,8},{10,11... | collective-permute-start | bytes 24584 | tf_op jit(solution)/shard_map/ppermute | solution.py:24
  74.2 5.2 %collective-permute-start.20 = (f32[16,128]{1,0:T(8,128)S(1)}, f32[16,128]{1,0:T(8,128)S(1)}, u32[]{:S(2)}, u32[]{:S(2)}) collective-permute-start(f32[16,128]{1,0:T(8,128)S(1)} %multiply_add_fusion.1.refs_0_), channel_id=1, source_target_pairs={{0,4},{2,6},{4,0},{6,2},{1,5},{3,7},{5,1},{7,3},{8,12},{10,14},{12... | collective-permute-start | bytes 24584 | tf_op jit(solution)/shard_map/ppermute | solution.py:24
  75.4 4.0 %collective-permute-start.19 = (f32[16,128]{1,0:T(8,128)S(1)}, f32[16,128]{1,0:T(8,128)S(1)}, u32[]{:S(2)}, u32[]{:S(2)}) collective-permute-start(f32[16,128]{1,0:T(8,128)S(1)} %multiply_add_fusion.1.refs_0_), channel_id=1, source_target_pairs={{0,2},{2,4},{4,6},{6,0},{1,3},{3,5},{5,7},{7,1},{8,10},{10,12},{12... | collective-permute-start | bytes 24584 | tf_op jit(solution)/shard_map/ppermute | solution.py:24
  77.7 4.9 %collective-permute-start.18 = (f32[16,128]{1,0:T(8,128)S(1)}, f32[16,128]{1,0:T(8,128)S(1)}, u32[]{:S(2)}, u32[]{:S(2)}) collective-permute-start(f32[16,128]{1,0:T(8,128)S(1)} %multiply_add_fusion.1.refs_0_), channel_id=1, source_target_pairs={{0,6},{2,0},{4,2},{6,4},{1,7},{3,1},{5,3},{7,5},{8,14},{10,8},{12,... | collective-permute-start | bytes 24584 | tf_op jit(solution)/shard_map/ppermute | solution.py:24
  91.0 5.5 %collective-permute-start.23 = (f32[32,128]{1,0:T(8,128)S(1)}, f32[32,128]{1,0:T(8,128)S(1)}, u32[]{:S(2)}, u32[]{:S(2)}) collective-permute-start(f32[32,128]{1,0:T(8,128)S(1)} %get-tuple-element.39), channel_id=1, source_target_pairs={{0,16},{8,24},{16,0},{24,8},{1,17},{9,25},{17,1},{25,9},{2,18},{10... | collective-permute-start | bytes 49160 | tf_op jit(solution)/shard_map/ppermute | solution.py:24
  91.8 5.5 %collective-permute-start.22 = (f32[32,128]{1,0:T(8,128)S(1)}, f32[32,128]{1,0:T(8,128)S(1)}, u32[]{:S(2)}, u32[]{:S(2)}) collective-permute-start(f32[32,128]{1,0:T(8,128)S(1)} %get-tuple-element.39), channel_id=1, source_target_pairs={{0,8},{8,16},{16,24},{24,0},{1,9},{9,17},{17,25},{25,1},{2,10},{10... | collective-permute-start | bytes 49160 | tf_op jit(solution)/shard_map/ppermute | solution.py:24
  95.9 3.7 %collective-permute-start.21 = (f32[32,128]{1,0:T(8,128)S(1)}, f32[32,128]{1,0:T(8,128)S(1)}, u32[]{:S(2)}, u32[]{:S(2)}) collective-permute-start(f32[32,128]{1,0:T(8,128)S(1)} %get-tuple-element.39), channel_id=1, source_target_pairs={{0,24},{8,0},{16,8},{24,16},{1,25},{9,1},{17,9},{25,17},{2,26},{10... | collective-permute-start | bytes 49160 | tf_op jit(solution)/shard_map/ppermute | solution.py:24
